TPU v7x, 32 devices: a whole 2x2x4 slice. The times are simulated.
32 devices in a mesh: gx: 4 (over z), gy: 4 (over x, core), gz: 2 (over y).
Axes of the slice: x: 2, y: 2, z: 4, core: 2. Of those that a mesh axis runs over, the one named last changes fastest.
Arguments:
- populations: float32 [19, 32, 32, 256], P(None, 'gx', 'gy', 'gz'), as said below
- solid: int32 [32, 32, 256], P('gx', 'gy', 'gz'), may hold values 0 or 1
- marker_pos: float32 [256, 3, 128], P(('gx', 'gy', 'gz')), may hold values from 2 to 125, as said below
- anchor_offset: float32 [256, 3, 128], P(('gx', 'gy', 'gz')), may hold values from -3 to 3
- links: int32 [256, 2, 128], P(('gx', 'gy', 'gz')), may hold values from 0 to 127
- patch_col: int32 [256, 1], P(('gx', 'gy', 'gz')), may hold values from 0 to 3; in each aligned block of 8 rows (0 to 7, 8 to 15, ...) at most 4 rows name the same one
Outputs:
- new_populations: float32 [19, 32, 32, 256], P(None, 'gx', 'gy', 'gz')
- marker_shift: float32 [256, 3, 128], P(('gx', 'gy', 'gz'))
Inputs may be any that keep to these rules, and one draw needn't show every extreme that they name: `marker_pos`: each marker lies from 2 to 5 cells along the first coordinate of its patch, 2 to 5 along the second, 2 to 125 along the third. `patch_col`: among the 8 blocks of one device no patch index is named more than 4 times. `populations`: every population is positive.
All inputs are finite; a program needn't handle non-finite values. No bound on the sum of `solid` on one device may be relied on, other than what follows from the above.
Results may differ from a plain program's by a relative error of at most 0.00035.
Values sent between devices are 32-bit elements; how exact they have to be, the bound alone decides.
A program may use at most 64 MiB of HBM per device.

v0:
```python
import functools

import jax
import jax.numpy as jnp
from jax import lax
from jax.experimental import pallas as pl
from jax.experimental.pallas import tpu as pltpu
from jax.sharding import PartitionSpec as P

STEPS = 3
VELOCITY = (
    (0, 0, 0), (1, 0, 0), (-1, 0, 0), (0, 1, 0), (0, -1, 0), (0, 0, 1), (0, 0, -1),
    (1, 1, 0), (-1, -1, 0), (1, -1, 0), (-1, 1, 0), (1, 0, 1), (-1, 0, -1), (1, 0, -1),
    (-1, 0, 1), (0, 1, 1), (0, -1, -1), (0, 1, -1), (0, -1, 1),
)
WEIGHTS = (1.0 / 3.0,) + (1.0 / 18.0,) * 6 + (1.0 / 36.0,) * 12
OPPOSITE = (0, 2, 1, 4, 3, 6, 5, 8, 7, 10, 9, 12, 11, 14, 13, 16, 15, 18, 17)
TAU = 0.8
K_TETHER = 0.05
K_SPRING = 0.1
NUMBER = {c: q for q, c in enumerate(VELOCITY)}
ORDER = (
    [q for q in range(19) if VELOCITY[q][0] == 0]
    + [q for q in range(19) if VELOCITY[q][0] == 1]
    + [q for q in range(19) if VELOCITY[q][0] == -1]
)
PLACE = {q: i for i, q in enumerate(ORDER)}
Y_MOVERS = [
    [NUMBER[(0, s, 0)], NUMBER[(1, s, 0)], NUMBER[(-1, s, 0)], NUMBER[(0, s, 1)], NUMBER[(0, s, -1)]]
    for s in (1, -1)
]
Z_MOVERS = [
    [NUMBER[(0, 0, s)], NUMBER[(1, 0, s)], NUMBER[(-1, 0, s)], NUMBER[(0, 1, s)], NUMBER[(0, -1, s)]]
    for s in (1, -1)
]
MESH = pl.DeviceIdType.MESH
PARK = -1000.0
HALF = 64


def axis_sum(values, column):
    total = None
    for q in range(19):
        sign = VELOCITY[q][column]
        if sign == 0:
            continue
        term = values[q]
        total = (term if sign == 1 else -term) if total is None else (
            total + term if sign == 1 else total - term
        )
    return total


def moments(f):
    density = f[0]
    for q in range(1, 19):
        density = density + f[q]
    return density, [axis_sum(f, column) for column in range(3)]


def project(vector, direction):
    total = None
    for column in range(3):
        if direction[column]:
            term = vector[column] if direction[column] == 1 else -vector[column]
            total = term if total is None else total + term
    return total


def collide(f, density, momentum, field, wall):
    over = 1.0 / density
    omega = 1.0 / TAU
    factor = 1.0 - 0.5 / TAU
    if field is None:
        u = [momentum[k] * over for k in range(3)]
    else:
        u = [(momentum[k] + 0.5 * field[k]) * over for k in range(3)]
    square = u[0] * u[0] + u[1] * u[1] + u[2] * u[2]
    base = omega * density * (1.0 - 1.5 * square)
    if field is not None:
        power = u[0] * field[0] + u[1] * field[1] + u[2] * field[2]
        base = base - (3.0 * factor) * power
    scaled = omega * density
    post = [None] * 19
    rest = (1.0 - omega) * f[0] + WEIGHTS[0] * base
    post[0] = jnp.where(wall, f[0], rest)
    for q in range(1, 19, 2):
        p = OPPOSITE[q]
        along = project(u, VELOCITY[q])
        flow = scaled * along
        inner = 4.5 * flow
        odd = 3.0 * flow
        if field is not None:
            pushed = project(field, VELOCITY[q])
            inner = inner + (9.0 * factor) * pushed
            odd = odd + (3.0 * factor) * pushed
        even = WEIGHTS[q] * (base + along * inner)
        odd = WEIGHTS[q] * odd
        post[q] = jnp.where(wall, f[p], (1.0 - omega) * f[q] + (even + odd))
        post[p] = jnp.where(wall, f[q], (1.0 - omega) * f[p] + (even - odd))
    return post


def kernel(
    sizes,
    pop, solid, mpos, moff, links, pcol,
    outf, outs,
    post, ysend, yhalo, zsend, zhalo, zin, mom, gfield, vsplit,
    msend, mrecv, disp, dback, where_to, terms, pz, plane,
    msend_sem, mrecv_sem, hsend_sem, hrecv_sem, bsend_sem, brecv_sem,
):
    nx, ny, nz, blocks, cap, cx = sizes
    slots = nx * cap
    gx, gy, gz = lax.axis_index("gx"), lax.axis_index("gy"), lax.axis_index("gz")
    right, left = lax.rem(gx + 1, nx), lax.rem(gx + nx - 1, nx)
    up, down = lax.rem(gy + 1, ny), lax.rem(gy + ny - 1, ny)
    other = lax.rem(gz + 1, nz)

    barrier = pltpu.get_barrier_semaphore()
    near = [(gx, up, gz), (gx, down, gz), (gx, gy, other)]
    near += [(a, b, gz) for a in (right, left) for b in (up, down)]
    near += [(right, gy, other), (left, gy, other), (gx, up, other), (gx, down, other)]
    for o in range(1, nx):
        near.append((lax.rem(gx + o, nx), gy, gz))
    for device in near:
        pl.semaphore_signal(barrier, inc=1, device_id=device, device_id_type=MESH)

    row = lax.broadcasted_iota(jnp.int32, (8, 128), 0)
    lane = lax.broadcasted_iota(jnp.int32, (8, 128), 1)

    columns = jnp.broadcast_to(pcol[...], (blocks, 128))
    named = [jnp.broadcast_to(columns[b : b + 1, :], (8, 128)) for b in range(blocks)]
    spots = []
    for b in range(blocks):
        spot = named[b] * cap
        for e in range(b):
            spot = spot + jnp.where(named[e] == named[b], 1, 0)
        spots.append(spot)
        where_to[b] = spot
    tiles = []
    for b in range(blocks):
        tiles.append(
            jnp.concatenate([mpos[b], moff[b], links[b].astype(jnp.float32)], axis=0)
        )
    empty = jnp.where(row < 3, PARK, 0.0)
    for s in range(slots):
        tile = empty
        for b in range(blocks):
            tile = jnp.where(spots[b] == s, tiles[b], tile)
        msend[s] = tile

    pl.semaphore_wait(barrier, len(near))

    def exchange(source, target, send_sem, recv_sem):
        copies = []
        for o in range(1, nx):
            to = lax.rem(gx + o, nx)
            copy = pltpu.make_async_remote_copy(
                src_ref=source.at[pl.ds(to * cap, cap)],
                dst_ref=target.at[pl.ds(gx * cap, cap)],
                send_sem=send_sem.at[o],
                recv_sem=recv_sem.at[o],
                device_id=(to, gy, gz),
                device_id_type=MESH,
            )
            copy.start()
            copies.append(copy)
        for k in range(cap):
            target[gx * cap + k] = source[gx * cap + k]
        return copies

    marker_copies = exchange(msend, mrecv, msend_sem, mrecv_sem)

    def halo(step):
        copies = []

        def go(source, target, device):
            n = len(copies)
            copy = pltpu.make_async_remote_copy(
                src_ref=source,
                dst_ref=target,
                send_sem=hsend_sem.at[step, n],
                recv_sem=hrecv_sem.at[step, n],
                device_id=device,
                device_id_type=MESH,
            )
            copy.start()
            copies.append(copy)

        z = zsend.at[step]
        go(z, zhalo.at[step, 1], (right, gy, other))
        go(z, zhalo.at[step, 2], (left, gy, other))
        go(z, zhalo.at[step, 3], (gx, up, other))
        go(z, zhalo.at[step, 4], (gx, down, other))
        for d, b in ((0, up), (1, down)):
            for j, x, a in ((1, cx - 1, right), (2, 0, left)):
                go(
                    ysend.at[step, d, j, pl.ds(x, 1)],
                    yhalo.at[step, d, j, pl.ds(cx, 1)],
                    (a, b, gz),
                )
        go(post.at[step, pl.ds(9, 5), cx], post.at[step, pl.ds(9, 5), 0], (right, gy, gz))
        go(post.at[step, pl.ds(14, 5), 1], post.at[step, pl.ds(14, 5), cx + 1], (left, gy, gz))
        go(ysend.at[step, 0], yhalo.at[step, 0, :, pl.ds(0, cx)], (gx, up, gz))
        go(ysend.at[step, 1], yhalo.at[step, 1, :, pl.ds(0, cx)], (gx, down, gz))
        go(z, zhalo.at[step, 0], (gx, gy, other))
        return copies

    def emit(step, x, values):
        for q in range(19):
            post[step, PLACE[q], x + 1] = values[q]

    def rim(step, x, values, packed):
        for d, edge in ((0, 7), (1, 0)):
            for j, q in enumerate(Y_MOVERS[d]):
                ysend[step, d, j, pl.ds(x, 1)] = values[q][edge : edge + 1, :]
        for d, edge in ((0, 127), (1, 0)):
            for j, q in enumerate(Z_MOVERS[d]):
                column = jnp.broadcast_to(values[q][:, edge : edge + 1], (8, 128))
                packed = jnp.where(lane == x + (d * HALF + j * 8), column, packed)
        return packed

    def stream(step, x, last):
        turned = pltpu.roll(zin[...], lax.rem(128 - x, 128), axis=1)
        f = []
        for q in range(19):
            c = VELOCITY[q]
            tile = post[step, PLACE[q], x + 1 - c[0]]
            if c[1]:
                d = 0 if c[1] == 1 else 1
                j = Y_MOVERS[d].index(q)
                if c[0] == 1:
                    at = lax.rem(x + cx, cx + 1)
                else:
                    at = x - c[0]
                line = jnp.broadcast_to(yhalo[step, d, j, pl.ds(at, 1)], (8, 128))
                tile = jnp.where(row == (0 if d == 0 else 7), line, pltpu.roll(tile, 1 if d == 0 else 7, axis=0))
            if c[2]:
                d = 0 if c[2] == 1 else 1
                j = Z_MOVERS[d].index(q)
                k = d * HALF + j * 8
                column = jnp.broadcast_to(turned[:, k : k + 1], (8, 128))
                tile = jnp.where(
                    lane == (0 if d == 0 else 127), column, pltpu.roll(tile, 1 if d == 0 else 127, axis=1)
                )
            f.append(tile)
            outf[q, x] = tile
        density, momentum = moments(f)
        mom[0, x] = density
        over = 1.0 / density
        for k in range(3):
            mom[k + 1, x] = momentum[k]
            v = momentum[k] * over
            gfield[k, x] = v

    def combine(step):
        face = zhalo[step, 0]
        group = lax.rem(lane, HALF) // 8
        inside = lax.rem(lane, 8)
        forward = jnp.where(
            inside == 0, pltpu.roll(zhalo[step, 1], 121, axis=1), pltpu.roll(face, 1, axis=1)
        )
        backward = jnp.where(
            inside == 7, pltpu.roll(zhalo[step, 2], 7, axis=1), pltpu.roll(face, 127, axis=1)
        )
        rising = jnp.where(
            row == 0, pltpu.roll(zhalo[step, 3], 1, axis=0), pltpu.roll(face, 1, axis=0)
        )
        falling = jnp.where(
            row == 7, pltpu.roll(zhalo[step, 4], 7, axis=0), pltpu.roll(face, 7, axis=0)
        )
        zin[...] = jnp.where(
            group == 0,
            face,
            jnp.where(
                group == 1,
                forward,
                jnp.where(group == 2, backward, jnp.where(group == 3, rising, falling)),
            ),
        )

    def spread(step):
        depth = lax.broadcasted_iota(jnp.int32, (128, 128), 0).astype(jnp.float32)
        cell = row.astype(jnp.float32)

        def one(s, carry):
            info = mrecv[s]
            if step == 0:
                shift = jnp.zeros((8, 128), jnp.float32)
                disp[s] = shift
            else:
                shift = disp[s]
            position = info + shift
            rest_to_anchor = pltpu.roll(info, 5, axis=0)
            force = K_TETHER * ((info + rest_to_anchor) - position)
            if step > 0:
                for k in range(2):
                    index = jnp.broadcast_to(info[6 + k : 7 + k, :], (8, 128)).astype(jnp.int32)
                    chosen = jnp.take_along_axis(shift, index, axis=1)
                    force = force + K_SPRING * (chosen - shift)
            at = pl.ds(pl.multiple_of(s * 128, 128), 128)
            wz = jnp.maximum(0.0, 1.0 - jnp.abs(position[2:3, :] - depth))
            high = wz.astype(jnp.bfloat16)
            pz[0:128, at] = high
            pz[128:256, at] = (wz - high.astype(jnp.float32)).astype(jnp.bfloat16)
            wx = jnp.maximum(0.0, 1.0 - jnp.abs(position[0:1, :] - cell))
            wy = jnp.maximum(0.0, 1.0 - jnp.abs(position[1:2, :] - cell))
            full = jnp.concatenate([wx[i : i + 1, :] * wy for i in range(8)], axis=0)
            plane[:, at] = full
            for k in range(3):
                term = force[k : k + 1, :] * full
                high = term.astype(jnp.bfloat16)
                terms[k * 64 : k * 64 + 64, at] = high
                terms[192 + k * 64 : 256 + k * 64, at] = (
                    term - high.astype(jnp.float32)
                ).astype(jnp.bfloat16)
            return carry

        lax.fori_loop(0, slots, one, 0)
        product = lax.dot_general(
            terms[...], pz[...], (((1,), (1,)), ((), ())), preferred_element_type=jnp.float32
        )
        total = product[0:192, 0:128] + (product[0:192, 128:256] + product[192:384, 0:128])
        gfield[...] = total.reshape(3, 8, 8, 128)

    def sample():
        v = gfield[...].reshape(192, 128)
        high = v.astype(jnp.bfloat16)
        low = (v - high.astype(jnp.float32)).astype(jnp.bfloat16)
        vsplit[0:192, 0:128] = high
        vsplit[0:192, 128:256] = high
        vsplit[192:384, 0:128] = low
        vsplit[192:384, 128:256] = low

        def pair(i, carry):
            at = pl.ds(pl.multiple_of(i * 256, 256), 256)
            product = jnp.dot(vsplit[...], pz[:, at], preferred_element_type=jnp.float32)
            full = plane[:, at]
            for k in range(3):
                part = (product[k * 64 : k * 64 + 64] + product[192 + k * 64 : 256 + k * 64]) * full
                moved = jnp.sum(part, axis=0, keepdims=True)
                for h in range(2):
                    disp[2 * i + h, k : k + 1, :] = (
                        disp[2 * i + h, k : k + 1, :] + moved[:, h * 128 : h * 128 + 128]
                    )
            return carry

        lax.fori_loop(0, slots // 2, pair, 0)

    def first(x, packed):
        f = [pop[q, x] for q in range(19)]
        density, momentum = moments(f)
        mom[0, x] = density
        for k in range(3):
            mom[k + 1, x] = momentum[k]
        values = collide(f, density, momentum, None, solid[x] == 1)
        emit(0, x, values)
        return rim(0, x, values, packed)

    zsend[0] = lax.fori_loop(0, cx, first, jnp.zeros((8, 128), jnp.float32))
    halos = [halo(0)]
    for copy in marker_copies:
        copy.wait_recv()
    spread(0)

    def driven(x, carry):
        f = [pop[q, x] for q in range(19)]
        values = collide(
            f, mom[0, x], [mom[k, x] for k in range(1, 4)], [gfield[k, x] for k in range(3)],
            solid[x] == 1,
        )
        emit(0, x, values)
        return carry

    lax.fori_loop(2, cx - 2, driven, 0)

    for step in range(STEPS):
        if step > 0:
            spread(step)

            def coupled(x, packed):
                f = [outf[q, x] for q in range(19)]
                values = collide(
                    f, mom[0, x], [mom[k, x] for k in range(1, 4)],
                    [gfield[k, x] for k in range(3)], solid[x] == 1,
                )
                emit(step, x, values)
                return rim(step, x, values, packed)

            zsend[step] = lax.fori_loop(0, cx, coupled, jnp.zeros((8, 128), jnp.float32))
            halos.append(halo(step))
        for copy in halos[step]:
            copy.wait_recv()
        combine(step)

        def moving(x, carry):
            stream(step, x, step == STEPS - 1)
            return carry

        lax.fori_loop(0, cx, moving, 0)
        sample()

    back_copies = exchange(disp, dback, bsend_sem, brecv_sem)
    for copy in back_copies:
        copy.wait_recv()
    for b in range(blocks):
        tile = jnp.zeros((8, 128), jnp.float32)
        spot = where_to[b]
        for s in range(slots):
            tile = jnp.where(spot == s, dback[s], tile)
        outs[b] = tile[0:3, :]
    for copies in [marker_copies] + halos + [back_copies]:
        for copy in copies:
            copy.wait_send()


def shards(sizes, populations, solid, marker_pos, anchor_offset, links, patch_col):
    nx, ny, nz, blocks, cap, cx = sizes
    slots = nx * cap
    f32 = jnp.float32
    tile = (8, 128)
    vmem = pl.BlockSpec(memory_space=pltpu.VMEM)
    dma = pltpu.SemaphoreType.DMA
    return pl.pallas_call(
        functools.partial(kernel, sizes),
        out_shape=(
            jax.ShapeDtypeStruct(populations.shape, f32),
            jax.ShapeDtypeStruct(marker_pos.shape, f32),
        ),
        in_specs=[vmem] * 6,
        out_specs=(vmem, vmem),
        scratch_shapes=[
            pltpu.VMEM((STEPS, 19, cx + 2) + tile, f32),
            pltpu.VMEM((STEPS, 2, 5) + tile, f32),
            pltpu.VMEM((STEPS, 2, 5, 16, 128), f32),
            pltpu.VMEM((STEPS,) + tile, f32),
            pltpu.VMEM((STEPS, 5) + tile, f32),
            pltpu.VMEM(tile, f32),
            pltpu.VMEM((4, cx) + tile, f32),
            pltpu.VMEM((3, cx) + tile, f32),
            pltpu.VMEM((384, 256), jnp.bfloat16),
            pltpu.VMEM((slots,) + tile, f32),
            pltpu.VMEM((slots,) + tile, f32),
            pltpu.VMEM((slots,) + tile, f32),
            pltpu.VMEM((slots,) + tile, f32),
            pltpu.VMEM((blocks,) + tile, jnp.int32),
            pltpu.VMEM((384, slots * 128), jnp.bfloat16),
            pltpu.VMEM((256, slots * 128), jnp.bfloat16),
            pltpu.VMEM((64, slots * 128), f32),
            dma((nx,)), dma((nx,)),
            dma((STEPS, 13)), dma((STEPS, 13)),
            dma((nx,)), dma((nx,)),
        ],
        compiler_params=pltpu.CompilerParams(
            collective_id=0, has_side_effects=True, vmem_limit_bytes=40 * 1024 * 1024
        ),
    )(populations, solid, marker_pos, anchor_offset, links, patch_col)


def solution(mesh):
    placed = (
        P(None, "gx", "gy", "gz"),
        P("gx", "gy", "gz"),
        P(("gx", "gy", "gz"), None, None),
        P(("gx", "gy", "gz"), None, None),
        P(("gx", "gy", "gz"), None, None),
        P(("gx", "gy", "gz"), None),
    )

    def whole(populations, solid, marker_pos, anchor_offset, links, patch_col):
        nx, ny, nz = (mesh.shape[name] for name in ("gx", "gy", "gz"))
        blocks = marker_pos.shape[0] // (nx * ny * nz)
        cap = max(2, 2 * blocks // nx)
        sizes = (nx, ny, nz, blocks, cap, populations.shape[1] // nx)
        return jax.shard_map(
            functools.partial(shards, sizes),
            mesh=mesh,
            in_specs=placed,
            out_specs=(P(None, "gx", "gy", "gz"), P(("gx", "gy", "gz"), None, None)),
            check_vma=False,
        )(populations, solid, marker_pos, anchor_offset, links, patch_col)

    return whole
```

profile of v0, /device:TPU:0, one launch (start us, length us, event | category | flops | bytes accessed | tf_op | source)
XLA Modules:
  0.0 46.6 jit_solution(17426658234674848169)
XLA Ops:
  0.6 0.0 copy-start.1
  0.6 0.7 %copy.10.pcol = s32[8,1]{1,0:T(8,128)S(1)} copy(s32[8,1]{0,1:T(1,128)} %param.11) | data formatting | bytes 64 | tf_op args[5]
  1.4 0.7 %copy.8.mpos = f32[8,3,128]{2,1,0:T(4,128)S(1)} copy(f32[8,3,128]{2,0,1:T(8,128)} %param.8) | data formatting | bytes 24576 | tf_op args[2]
  2.1 0.0 copy-start.2
  2.1 0.7 %copy.9.moff = f32[8,3,128]{2,1,0:T(4,128)S(1)} copy(f32[8,3,128]{2,0,1:T(8,128)} %param.9) | data formatting | bytes 24576 | tf_op args[3]
  2.8 0.0 copy-done.1
  2.8 0.0 copy-done.2
  2.8 0.0 copy-start
  2.8 1.1 %copy-done = f32[19,8,8,128]{3,2,1,0:T(8,128)S(1)} copy-done((f32[19,8,8,128]{3,2,1,0:T(8,128)S(1)}, f32[19,8,8,128]{3,2,1,0:T(8,128)}, u32[]{:S(2)}) %copy-start) | copy-done | bytes 622616
  3.9 41.2 %shard_map.77 = (f32[19,8,8,128]{3,2,1,0:T(8,128)S(1)}, f32[8,3,128]{2,1,0:T(4,128)S(1)}) custom-call(f32[19,8,8,128]{3,2,1,0:T(8,128)S(1)} %copy-done, s32[8,8,128]{2,1,0:T(8,128)S(1)} %copy-done.1, f32[8,3,128]{2,1,0:T(4,128)S(1)} %copy.8.mpos, f32[8,3,128]{2,1,0:T(4,128)S(1)} %copy.9.moff, s32[8,2,128]{2,1,0:T(2,128)S(1)} %copy-done.2, s32[8,1]{1,0:T(8,128)S(1)} %copy.10.pcol), custom_call_target="tpu_custom_call" | custom-call | tf_op jit(solution)/shard_map/pallas_call | solution.py:424
  45.1 0.6 %copy.11 = f32[8,3,128]{2,0,1:T(8,128)} copy(f32[8,3,128]{2,1,0:T(4,128)S(1)} %get-tuple-element.3) | data formatting | bytes 24576 | tf_op jit(solution)/shard_map/pallas_call | solution.py:424
  45.7 0.8 %copy.13 = f32[19,8,8,128]{3,2,1,0:T(8,128)} copy(f32[19,8,8,128]{3,2,1,0:T(8,128)S(1)} %get-tuple-element.6) | data formatting | bytes 1245184
Async XLA Ops:
  0.6 2.2 %copy-start.1 = (s32[8,8,128]{2,1,0:T(8,128)S(1)}, s32[8,8,128]{2,1,0:T(8,128)}, u32[]{:S(2)}) copy-start(s32[8,8,128]{2,1,0:T(8,128)} %solid.1) | copy-start | bytes 98308
  2.1 0.7 %copy-start.2 = (s32[8,2,128]{2,1,0:T(2,128)S(1)}, s32[8,2,128]{2,1,0:T(2,128)}, u32[]{:S(2)}) copy-start(s32[8,2,128]{2,1,0:T(2,128)} %links.1) | copy-start | bytes 24580
  2.8 1.1 %copy-start = (f32[19,8,8,128]{3,2,1,0:T(8,128)S(1)}, f32[19,8,8,128]{3,2,1,0:T(8,128)}, u32[]{:S(2)}) copy-start(f32[19,8,8,128]{3,2,1,0:T(8,128)} %pop.1) | copy-start | bytes 1867780
where the time goes:
time: 46.9 us; the launch traced here: 46.6 us
  Pallas kernels  41.2 us (88%)
  local copies, waits for them, and re-layouts  4.68 us (10%)
  between operations  0.66 us (1%)
    pallas_call x1, Pallas kernels, shards(): pl.pallas_call(functools.partial(kernel, sizes), out_shape=(jax.ShapeDtyp...  41.2 us
    unnamed x10, local copies, waits for them, and re-layouts  4.08 us

commit v1 on v0

--- a/solution.py
+++ b/solution.py
@@ -35,6 +35,9 @@
 ]
 MESH = pl.DeviceIdType.MESH
 PARK = -1000.0
+SPREAD_UNROLL = 16
+CELL_UNROLL = 8
+WIDE = 1024
 HALF = 64
 
 
@@ -103,11 +106,11 @@
 
 def kernel(
     sizes,
-    pop, solid, mpos, moff, links, pcol,
-    outf, outs,
+    pop_hbm, solid, mpos, moff, links, pcol,
+    outf, outs, pop,
     post, ysend, yhalo, zsend, zhalo, zin, mom, gfield, vsplit,
     msend, mrecv, disp, dback, where_to, terms, pz, plane,
-    msend_sem, mrecv_sem, hsend_sem, hrecv_sem, bsend_sem, brecv_sem,
+    pop_sem, msend_sem, mrecv_sem, hsend_sem, hrecv_sem, bsend_sem, brecv_sem,
 ):
     nx, ny, nz, blocks, cap, cx = sizes
     slots = nx * cap
@@ -116,6 +119,8 @@
     up, down = lax.rem(gy + 1, ny), lax.rem(gy + ny - 1, ny)
     other = lax.rem(gz + 1, nz)
 
+    fetch = pltpu.make_async_copy(pop_hbm, pop, pop_sem)
+    fetch.start()
     barrier = pltpu.get_barrier_semaphore()
     near = [(gx, up, gz), (gx, down, gz), (gx, gy, other)]
     near += [(a, b, gz) for a in (right, left) for b in (up, down)]
@@ -128,8 +133,7 @@
     row = lax.broadcasted_iota(jnp.int32, (8, 128), 0)
     lane = lax.broadcasted_iota(jnp.int32, (8, 128), 1)
 
-    columns = jnp.broadcast_to(pcol[...], (blocks, 128))
-    named = [jnp.broadcast_to(columns[b : b + 1, :], (8, 128)) for b in range(blocks)]
+    named = [jnp.broadcast_to(pcol[:, b : b + 1], (8, 128)) for b in range(blocks)]
     spots = []
     for b in range(blocks):
         spot = named[b] * cap
@@ -140,7 +144,12 @@
     tiles = []
     for b in range(blocks):
         tiles.append(
-            jnp.concatenate([mpos[b], moff[b], links[b].astype(jnp.float32)], axis=0)
+            jnp.concatenate(
+                [mpos[k, b : b + 1, :] for k in range(3)]
+                + [moff[k, b : b + 1, :] for k in range(3)]
+                + [links[b].astype(jnp.float32)],
+                axis=0,
+            )
         )
     empty = jnp.where(row < 3, PARK, 0.0)
     for s in range(slots):
@@ -279,7 +288,13 @@
             ),
         )
 
+    def reach(step):
+        return (2, cx - 2) if step == 0 else (0, cx)
+
     def spread(step):
+        x0, x1 = reach(step)
+        size = (x1 - x0) * 8
+        n = 3 * size
         depth = lax.broadcasted_iota(jnp.int32, (128, 128), 0).astype(jnp.float32)
         cell = row.astype(jnp.float32)
 
@@ -305,47 +320,47 @@
             pz[128:256, at] = (wz - high.astype(jnp.float32)).astype(jnp.bfloat16)
             wx = jnp.maximum(0.0, 1.0 - jnp.abs(position[0:1, :] - cell))
             wy = jnp.maximum(0.0, 1.0 - jnp.abs(position[1:2, :] - cell))
-            full = jnp.concatenate([wx[i : i + 1, :] * wy for i in range(8)], axis=0)
-            plane[:, at] = full
+            full = jnp.concatenate([wx[i : i + 1, :] * wy for i in range(x0, x1)], axis=0)
+            plane[0:size, at] = full
             for k in range(3):
                 term = force[k : k + 1, :] * full
                 high = term.astype(jnp.bfloat16)
-                terms[k * 64 : k * 64 + 64, at] = high
-                terms[192 + k * 64 : 256 + k * 64, at] = (
+                terms[k * size : k * size + size, at] = high
+                terms[n + k * size : n + k * size + size, at] = (
                     term - high.astype(jnp.float32)
                 ).astype(jnp.bfloat16)
             return carry
 
-        lax.fori_loop(0, slots, one, 0)
+        lax.fori_loop(0, slots, one, 0, unroll=SPREAD_UNROLL)
         product = lax.dot_general(
-            terms[...], pz[...], (((1,), (1,)), ((), ())), preferred_element_type=jnp.float32
-        )
-        total = product[0:192, 0:128] + (product[0:192, 128:256] + product[192:384, 0:128])
-        gfield[...] = total.reshape(3, 8, 8, 128)
-
-    def sample():
-        v = gfield[...].reshape(192, 128)
+            terms[0 : 2 * n], pz[...], (((1,), (1,)), ((), ())), preferred_element_type=jnp.float32
+        )
+        total = product[0:n, 0:128] + (product[0:n, 128:256] + product[n : 2 * n, 0:128])
+        gfield[:, x0:x1] = total.reshape(3, x1 - x0, 8, 128)
+
+    def sample(step):
+        x0, x1 = reach(step)
+        size = (x1 - x0) * 8
+        n = 3 * size
+        v = gfield[:, x0:x1].reshape(n, 128)
         high = v.astype(jnp.bfloat16)
         low = (v - high.astype(jnp.float32)).astype(jnp.bfloat16)
-        vsplit[0:192, 0:128] = high
-        vsplit[0:192, 128:256] = high
-        vsplit[192:384, 0:128] = low
-        vsplit[192:384, 128:256] = low
-
-        def pair(i, carry):
-            at = pl.ds(pl.multiple_of(i * 256, 256), 256)
-            product = jnp.dot(vsplit[...], pz[:, at], preferred_element_type=jnp.float32)
-            full = plane[:, at]
+        vsplit[0:n, 0:128] = high
+        vsplit[0:n, 128:256] = high
+        vsplit[n : 2 * n, 0:128] = low
+        vsplit[n : 2 * n, 128:256] = low
+        for i in range(slots * 128 // WIDE):
+            at = pl.ds(i * WIDE, WIDE)
+            product = jnp.dot(vsplit[0 : 2 * n], pz[:, at], preferred_element_type=jnp.float32)
+            full = plane[0:size, at]
             for k in range(3):
-                part = (product[k * 64 : k * 64 + 64] + product[192 + k * 64 : 256 + k * 64]) * full
-                moved = jnp.sum(part, axis=0, keepdims=True)
-                for h in range(2):
-                    disp[2 * i + h, k : k + 1, :] = (
-                        disp[2 * i + h, k : k + 1, :] + moved[:, h * 128 : h * 128 + 128]
+                part = product[k * size : k * size + size] + product[n + k * size : n + k * size + size]
+                moved = jnp.sum(part * full, axis=0, keepdims=True)
+                for h in range(WIDE // 128):
+                    slot = i * (WIDE // 128) + h
+                    disp[slot, k : k + 1, :] = (
+                        disp[slot, k : k + 1, :] + moved[:, h * 128 : h * 128 + 128]
                     )
-            return carry
-
-        lax.fori_loop(0, slots // 2, pair, 0)
 
     def first(x, packed):
         f = [pop[q, x] for q in range(19)]
@@ -357,7 +372,8 @@
         emit(0, x, values)
         return rim(0, x, values, packed)
 
-    zsend[0] = lax.fori_loop(0, cx, first, jnp.zeros((8, 128), jnp.float32))
+    fetch.wait()
+    zsend[0] = lax.fori_loop(0, cx, first, jnp.zeros((8, 128), jnp.float32), unroll=CELL_UNROLL)
     halos = [halo(0)]
     for copy in marker_copies:
         copy.wait_recv()
@@ -372,7 +388,7 @@
         emit(0, x, values)
         return carry
 
-    lax.fori_loop(2, cx - 2, driven, 0)
+    lax.fori_loop(2, cx - 2, driven, 0, unroll=CELL_UNROLL)
 
     for step in range(STEPS):
         if step > 0:
@@ -387,7 +403,7 @@
                 emit(step, x, values)
                 return rim(step, x, values, packed)
 
-            zsend[step] = lax.fori_loop(0, cx, coupled, jnp.zeros((8, 128), jnp.float32))
+            zsend[step] = lax.fori_loop(0, cx, coupled, jnp.zeros((8, 128), jnp.float32), unroll=CELL_UNROLL)
             halos.append(halo(step))
         for copy in halos[step]:
             copy.wait_recv()
@@ -397,8 +413,8 @@
             stream(step, x, step == STEPS - 1)
             return carry
 
-        lax.fori_loop(0, cx, moving, 0)
-        sample()
+        lax.fori_loop(0, cx, moving, 0, unroll=CELL_UNROLL)
+        sample(step)
 
     back_copies = exchange(disp, dback, bsend_sem, brecv_sem)
     for copy in back_copies:
@@ -408,7 +424,8 @@
         spot = where_to[b]
         for s in range(slots):
             tile = jnp.where(spot == s, dback[s], tile)
-        outs[b] = tile[0:3, :]
+        for k in range(3):
+            outs[k, b : b + 1, :] = tile[k : k + 1, :]
     for copies in [marker_copies] + halos + [back_copies]:
         for copy in copies:
             copy.wait_send()
@@ -421,15 +438,16 @@
     tile = (8, 128)
     vmem = pl.BlockSpec(memory_space=pltpu.VMEM)
     dma = pltpu.SemaphoreType.DMA
-    return pl.pallas_call(
+    new, shift = pl.pallas_call(
         functools.partial(kernel, sizes),
         out_shape=(
             jax.ShapeDtypeStruct(populations.shape, f32),
-            jax.ShapeDtypeStruct(marker_pos.shape, f32),
+            jax.ShapeDtypeStruct((3, blocks, 128), f32),
         ),
-        in_specs=[vmem] * 6,
+        in_specs=[pl.BlockSpec(memory_space=pltpu.HBM)] + [vmem] * 5,
         out_specs=(vmem, vmem),
         scratch_shapes=[
+            pltpu.VMEM(populations.shape, f32),
             pltpu.VMEM((STEPS, 19, cx + 2) + tile, f32),
             pltpu.VMEM((STEPS, 2, 5) + tile, f32),
             pltpu.VMEM((STEPS, 2, 5, 16, 128), f32),
@@ -447,14 +465,23 @@
             pltpu.VMEM((384, slots * 128), jnp.bfloat16),
             pltpu.VMEM((256, slots * 128), jnp.bfloat16),
             pltpu.VMEM((64, slots * 128), f32),
+            dma,
             dma((nx,)), dma((nx,)),
             dma((STEPS, 13)), dma((STEPS, 13)),
             dma((nx,)), dma((nx,)),
         ],
         compiler_params=pltpu.CompilerParams(
-            collective_id=0, has_side_effects=True, vmem_limit_bytes=40 * 1024 * 1024
+            collective_id=0, has_side_effects=True, vmem_limit_bytes=62 * 1024 * 1024
         ),
-    )(populations, solid, marker_pos, anchor_offset, links, patch_col)
+    )(
+        populations,
+        solid,
+        jnp.transpose(marker_pos, (1, 0, 2)),
+        jnp.transpose(anchor_offset, (1, 0, 2)),
+        links,
+        patch_col.T,
+    )
+    return new, jnp.transpose(shift, (1, 0, 2))
 
 
 def solution(mesh):

time: 46.9 us -> 35 us (0.75)
  Pallas kernels: 41.2 us -> 31.5 us
  local copies, waits for them, and re-layouts: 4.68 us -> 2.57 us
    pallas_call x1, Pallas kernels: 41.2 us -> 31.5 us  [shards(): pl.pallas_call(functools.partial(kernel, sizes), out_shape=(jax.ShapeDtyp...]
    unnamed x10 -> x4, local copies, waits for them, and re-layouts: 4.08 us -> 2.57 us
    pallas_call x1 -> x0, local copies, waits for them, and re-layouts: 0.6 us -> none  [shards(): pl.pallas_call(functools.partial(kernel, sizes), out_shape=(jax.ShapeDtyp...]
where the time goes in v1:
time: 35 us; the launch traced here: 34.8 us
  Pallas kernels  31.5 us (90%)
  local copies, waits for them, and re-layouts  2.57 us (7%)
  between operations  0.65 us (2%)
    pallas_call x1, Pallas kernels, shards(): pl.pallas_call(functools.partial(kernel, sizes), out_shape=(jax.ShapeDtyp...  31.5 us
    unnamed x4, local copies, waits for them, and re-layouts  2.57 us

profile of v1, /device:TPU:0, one launch (start us, length us, event | category | flops | bytes accessed | tf_op | source)
XLA Modules:
  0.0 34.8 jit_solution(331940803622446725)
XLA Ops:
  0.6 31.5 %shard_map.77 = (f32[19,8,8,128]{3,2,1,0:T(8,128)}, f32[3,8,128]{2,1,0:T(8,128)}) custom-call(f32[19,8,8,128]{3,2,1,0:T(8,128)} %pop_hbm.1, s32[8,8,128]{2,1,0:T(8,128)} %solid.1, f32[3,8,128]{2,1,0:T(8,128)} %bitcast.5, f32[3,8,128]{2,1,0:T(8,128)} %bitcast.6, s32[8,2,128]{2,1,0:T(2,128)} %links.1, s32[1,8]{1,0:T(1,128)} %bitcast.7), custom_call_target="tpu_custom_call" | custom-call | tf_op jit(solution)/shard_map/pallas_call | solution.py:441
  32.2 0.0 copy-start
  32.2 2.0 %copy.10 = f32[19,8,8,128]{3,2,1,0:T(8,128)} copy(f32[19,8,8,128]{3,2,1,0:T(8,128)} %get-tuple-element.8) | data formatting | bytes 1245184
  34.2 0.0 copy-done
  34.2 0.6 %copy.11 = f32[8,3,128]{2,0,1:T(8,128)} copy(f32[8,3,128]{2,0,1:T(8,128)S(1)} %bitcast.4) | data formatting | bytes 24576
Async XLA Ops:
  32.2 2.0 %copy-start = (f32[3,8,128]{2,1,0:T(8,128)S(1)}, f32[3,8,128]{2,1,0:T(8,128)}, u32[]{:S(2)}) copy-start(f32[3,8,128]{2,1,0:T(8,128)} %get-tuple-element.5) | copy-start | bytes 36868

commit v2 on v1

--- a/solution.py
+++ b/solution.py
@@ -109,7 +109,7 @@
     pop_hbm, solid, mpos, moff, links, pcol,
     outf, outs, pop,
     post, ysend, yhalo, zsend, zhalo, zin, mom, gfield, vsplit,
-    msend, mrecv, disp, dback, where_to, terms, pz, plane,
+    msend, mrecv, disp, dsend, dback, where_to, terms, pz, plane,
     pop_sem, msend_sem, mrecv_sem, hsend_sem, hrecv_sem, bsend_sem, brecv_sem,
 ):
     nx, ny, nz, blocks, cap, cx = sizes
@@ -160,13 +160,13 @@
 
     pl.semaphore_wait(barrier, len(near))
 
-    def exchange(source, target, send_sem, recv_sem):
+    def exchange(source, target, count, send_sem, recv_sem):
         copies = []
         for o in range(1, nx):
             to = lax.rem(gx + o, nx)
             copy = pltpu.make_async_remote_copy(
-                src_ref=source.at[pl.ds(to * cap, cap)],
-                dst_ref=target.at[pl.ds(gx * cap, cap)],
+                src_ref=source.at[pl.ds(to * count, count)],
+                dst_ref=target.at[pl.ds(gx * count, count)],
                 send_sem=send_sem.at[o],
                 recv_sem=recv_sem.at[o],
                 device_id=(to, gy, gz),
@@ -174,11 +174,11 @@
             )
             copy.start()
             copies.append(copy)
-        for k in range(cap):
-            target[gx * cap + k] = source[gx * cap + k]
+        for k in range(count):
+            target[gx * count + k] = source[gx * count + k]
         return copies
 
-    marker_copies = exchange(msend, mrecv, msend_sem, mrecv_sem)
+    marker_copies = exchange(msend, mrecv, cap, msend_sem, mrecv_sem)
 
     def halo(step):
         copies = []
@@ -416,14 +416,20 @@
         lax.fori_loop(0, cx, moving, 0, unroll=CELL_UNROLL)
         sample(step)
 
-    back_copies = exchange(disp, dback, bsend_sem, brecv_sem)
+    for i in range(slots // 2):
+        dsend[i] = disp[2 * i] + pltpu.roll(disp[2 * i + 1], 4, axis=0)
+    back_copies = exchange(dsend, dback, cap // 2, bsend_sem, brecv_sem)
     for copy in back_copies:
         copy.wait_recv()
     for b in range(blocks):
         tile = jnp.zeros((8, 128), jnp.float32)
+        half = jnp.zeros((8, 128), jnp.float32)
         spot = where_to[b]
-        for s in range(slots):
-            tile = jnp.where(spot == s, dback[s], tile)
+        for i in range(slots // 2):
+            pair = dback[i]
+            tile = jnp.where(spot == 2 * i, pair, tile)
+            half = jnp.where(spot == 2 * i + 1, pair, half)
+        tile = tile + pltpu.roll(half, 4, axis=0)
         for k in range(3):
             outs[k, b : b + 1, :] = tile[k : k + 1, :]
     for copies in [marker_copies] + halos + [back_copies]:
@@ -460,7 +466,8 @@
             pltpu.VMEM((slots,) + tile, f32),
             pltpu.VMEM((slots,) + tile, f32),
             pltpu.VMEM((slots,) + tile, f32),
-            pltpu.VMEM((slots,) + tile, f32),
+            pltpu.VMEM((slots // 2,) + tile, f32),
+            pltpu.VMEM((slots // 2,) + tile, f32),
             pltpu.VMEM((blocks,) + tile, jnp.int32),
             pltpu.VMEM((384, slots * 128), jnp.bfloat16),
             pltpu.VMEM((256, slots * 128), jnp.bfloat16),

time: 35 us -> 34.9 us (level)
  no operation moved by 1% of the time
where the time goes in v2:
time: 34.9 us; the launch traced here: 34.7 us
  Pallas kernels  31.5 us (90%)
  local copies, waits for them, and re-layouts  2.57 us (7%)
  between operations  0.65 us (2%)
    pallas_call x1, Pallas kernels, shards(): pl.pallas_call(functools.partial(kernel, sizes), out_shape=(jax.ShapeDtyp...  31.5 us
    unnamed x4, local copies, waits for them, and re-layouts  2.57 us

profile of v2, /device:TPU:0, one launch (start us, length us, event | category | flops | bytes accessed | tf_op | source)
XLA Modules:
  0.0 34.7 jit_solution(11466456076511939682)
XLA Ops:
  0.6 31.5 %shard_map.77 = (f32[19,8,8,128]{3,2,1,0:T(8,128)}, f32[3,8,128]{2,1,0:T(8,128)}) custom-call(f32[19,8,8,128]{3,2,1,0:T(8,128)} %pop_hbm.1, s32[8,8,128]{2,1,0:T(8,128)} %solid.1, f32[3,8,128]{2,1,0:T(8,128)} %bitcast.5, f32[3,8,128]{2,1,0:T(8,128)} %bitcast.6, s32[8,2,128]{2,1,0:T(2,128)} %links.1, s32[1,8]{1,0:T(1,128)} %bitcast.7), custom_call_target="tpu_custom_call" | custom-call | tf_op jit(solution)/shard_map/pallas_call | solution.py:447
  32.1 0.0 copy-start
  32.1 2.0 %copy.10 = f32[19,8,8,128]{3,2,1,0:T(8,128)} copy(f32[19,8,8,128]{3,2,1,0:T(8,128)} %get-tuple-element.8) | data formatting | bytes 1245184
  34.1 0.0 copy-done
  34.1 0.6 %copy.11 = f32[8,3,128]{2,0,1:T(8,128)} copy(f32[8,3,128]{2,0,1:T(8,128)S(1)} %bitcast.4) | data formatting | bytes 24576
Async XLA Ops:
  32.1 2.0 %copy-start = (f32[3,8,128]{2,1,0:T(8,128)S(1)}, f32[3,8,128]{2,1,0:T(8,128)}, u32[]{:S(2)}) copy-start(f32[3,8,128]{2,1,0:T(8,128)} %get-tuple-element.5) | copy-start | bytes 36868
